TPU v7x, 32 devices: a whole 2x2x4 slice. The times are simulated.
32 devices in a mesh: wide: 8 (over z, y), narrow: 4 (over x, core).
Axes of the slice: x: 2, y: 2, z: 4, core: 2. Of those that a mesh axis runs over, the one named last changes fastest.
Arguments:
- tokens: bfloat16 [80, 1024, 768], P('wide', 'narrow'), may hold values from -12 to 12, as said below
- usable: int32 [80, 1024], P('wide', 'narrow'), may hold values from 0 to 1, as said below
- conv_weight: bfloat16 [2304, 384], P(('wide', 'narrow')), may hold values from -0.125 to 0.125
- point_weight: bfloat16 [768, 384], P(('wide', 'narrow')), may hold values from -0.3125 to 0.3125
- head_weight: bfloat16 [768, 5313], P(('wide', 'narrow')), may hold values from -0.21875 to 0.21875
- first_gain: float32 [768], replicated, may hold values from 0.1 to 1.9
- first_shift: float32 [768], replicated, may hold values from -3 to 3
- second_gain: float32 [384], replicated, may hold values from 0.1 to 1.9
- second_shift: float32 [384], replicated, may hold values from -3 to 3
- point_bias: float32 [768], replicated, may hold values from -2 to 2
- head_bias: float32 [5313], replicated, may hold values from -1 to 1
- cot_block: bfloat16 [80, 1024, 768], P('wide', 'narrow'), may hold values from -6 to 6
- cot_tracks: bfloat16 [80, 5313, 1024], P('wide', None, 'narrow'), may hold values from -6 to 6
Outputs:
- block_out: bfloat16 [80, 1024, 768], P('wide', 'narrow')
- tracks_out: bfloat16 [80, 5313, 1024], P('wide', None, 'narrow')
- grad_tokens: float32 [80, 1024, 768], P('wide', 'narrow')
- grad_conv: float32 [2304, 384], P(('wide', 'narrow'))
- grad_point: float32 [768, 384], P(('wide', 'narrow'))
- grad_head: float32 [768, 5313], P(('wide', 'narrow'))
- grad_first_gain: float32 [768], replicated
- grad_first_shift: float32 [768], replicated
- grad_second_gain: float32 [384], replicated
- grad_second_shift: float32 [384], replicated
- grad_point_bias: float32 [768], replicated
- grad_head_bias: float32 [5313], replicated
Inputs may be any that keep to these rules, and one draw needn't show every extreme that they name: 1 marks a usable bin. Blacklisted runs of 16 aligned bins and scattered unmappable bins are 0, with a blacklist rate that differs from window to window; the first bin of every window is usable. `tokens`: activations of order one whose scale grows along the bins and windows.
All inputs are finite; a program needn't handle non-finite values.
Results may differ from a plain program's by a relative error of at most 0.008.
Values may be sent and summed in bfloat16 or wider, within the bound.
No kernel may reach another device: no remote copies, remote signals or barrier semaphores. Data moves between devices by JAX's collectives and lax.ppermute only.
A program may use at most 256 MiB of HBM per device.

v0:
```python
import jax
import jax.numpy as jnp
from jax import lax
from jax.sharding import PartitionSpec as P

DILATION_STEP = 11
epsilon = 1e-05


def with_halo(shard, sides, width):
    for axis, dim in sides:
        count, length = (lax.axis_size(axis), shard.shape[dim])
        up = [(i, (i + 1) % count) for i in range(count - 1)]
        down = [(j, i) for i, j in up]
        last = lax.slice_in_dim(shard, length - width, length, axis=dim)
        first = lax.slice_in_dim(shard, 0, width, axis=dim)
        before = lax.ppermute(last, axis, up)
        after = lax.ppermute(first, axis, down)
        shard = jnp.concatenate([before, shard, after], axis=dim)
    return shard


def norm_stats(values, weight):
    totals, counted = lax.psum(
        (jnp.sum(values * weight, axis=(0, 1)), jnp.sum(weight)), ("wide", "narrow")
    )
    mean_value = totals / counted
    centred = values - mean_value
    spread = lax.psum(jnp.sum(weight * centred * centred, axis=(0, 1)), ("wide", "narrow"))
    variance = spread / counted
    return (mean_value, lax.rsqrt(variance + epsilon), counted)


def convolve(padded_input, convolution_kernel, local_bin_count):
    hidden_state = jnp.einsum(
        "ldo,ov->ldv",
        padded_input[:, 0:local_bin_count],
        convolution_kernel[0],
        preferred_element_type=jnp.float32,
    )
    for kernel_position in range(1, 3):
        hidden_state = hidden_state + jnp.einsum(
            "ldo,ov->ldv",
            padded_input[
                :,
                kernel_position * DILATION_STEP : kernel_position * DILATION_STEP + local_bin_count,
            ],
            convolution_kernel[kernel_position],
            preferred_element_type=jnp.float32,
        )
    return hidden_state


def gelu_back(preact, upstream):
    return jax.vjp(jax.nn.gelu, preact)[1](upstream)[0]


def norm_back(grad_inner, normed, scale_inv, gain, grad_gain, grad_shift, weight, counted):
    grad_normed = grad_inner * gain
    return scale_inv * (
        grad_normed - weight / counted * (gain * grad_shift + normed * gain * grad_gain)
    )


def shards(
    tokens,
    usable,
    conv_weight,
    point_weight,
    head_weight,
    first_gain,
    first_shift,
    second_gain,
    second_shift,
    point_bias,
    head_bias,
    cot_block,
    cot_tracks,
):
    local_bin_count = tokens.shape[1]
    weight = usable.astype(jnp.float32)[:, :, None]
    row_weight = usable.astype(jnp.float32)[:, None, :]
    source = tokens.astype(jnp.float32)
    conv_full, point_full = (
        lax.all_gather(conv_weight, ("wide", "narrow"), axis=0, tiled=True),
        lax.all_gather(point_weight, ("wide", "narrow"), axis=0, tiled=True),
    )
    first_mean, first_scale, counted = norm_stats(source, weight)
    first_normed = (source - first_mean) * first_scale
    first_inner = first_normed * first_gain + first_shift
    first_activated = jax.nn.gelu(first_inner).astype(jnp.bfloat16)
    padded_input = with_halo(first_activated, (("narrow", 1),), DILATION_STEP)
    convolution_kernel = conv_full.reshape(3, -1, conv_full.shape[1])
    hidden_state = convolve(padded_input, convolution_kernel, local_bin_count)
    second_mean, second_scale, counted_two = norm_stats(hidden_state, weight)
    second_normed = (hidden_state - second_mean) * second_scale
    second_inner = second_normed * second_gain + second_shift
    second_active = jax.nn.gelu(second_inner).astype(jnp.bfloat16)
    branch = (
        jnp.einsum("wbh,ch->wbc", second_active, point_full, preferred_element_type=jnp.float32)
        + point_bias
    )
    block = (source + branch).astype(jnp.bfloat16)
    window_part = block
    logits = jnp.einsum(
        "wbc,ct->wtb",
        window_part,
        lax.all_gather(head_weight, ("wide", "narrow"), axis=0, tiled=True),
        preferred_element_type=jnp.float32,
    )
    logits = logits + head_bias[None, :, None]
    tracks = jax.nn.softplus(logits).astype(jnp.bfloat16)
    grad_logits = (cot_tracks.astype(jnp.float32) * row_weight * jax.nn.sigmoid(logits)).astype(
        jnp.bfloat16
    )
    grad_block = jnp.einsum(
        "wtb,ct->wbc",
        grad_logits,
        lax.all_gather(head_weight, ("wide", "narrow"), axis=0, tiled=True),
        preferred_element_type=jnp.float32,
    )
    window_part = block
    grad_head = lax.psum_scatter(
        jnp.einsum("wbc,wtb->ct", window_part, grad_logits, preferred_element_type=jnp.float32),
        ("wide", "narrow"),
        scatter_dimension=0,
        tiled=True,
    )
    grad_summed = cot_block.astype(jnp.float32) * weight + grad_block
    grad_branch = grad_summed.astype(jnp.bfloat16)
    conv_full, point_full = (
        lax.all_gather(conv_weight, ("wide", "narrow"), axis=0, tiled=True),
        lax.all_gather(point_weight, ("wide", "narrow"), axis=0, tiled=True),
    )
    convolution_kernel = conv_full.reshape(3, -1, conv_full.shape[1])
    first_normed = (source - first_mean) * first_scale
    first_inner = first_normed * first_gain + first_shift
    hidden_state = convolve(padded_input, convolution_kernel, local_bin_count)
    second_normed = (hidden_state - second_mean) * second_scale
    second_inner = second_normed * second_gain + second_shift
    second_active = jax.nn.gelu(second_inner).astype(jnp.bfloat16)
    grad_point_local = jnp.einsum(
        "wbc,wbh->ch", grad_branch, second_active, preferred_element_type=jnp.float32
    )
    grad_second_active = jnp.einsum(
        "ldo,ov->ldv", grad_branch, point_full, preferred_element_type=jnp.float32
    )
    grad_second_inner = gelu_back(second_inner, grad_second_active)
    bias_point_local = jnp.sum(grad_branch.astype(jnp.float32), axis=(0, 1))
    bias_head_local = jnp.sum(grad_logits.astype(jnp.float32), axis=(0, 2))
    grad_second_gain, grad_second_shift, grad_point_bias, grad_head_bias = lax.psum(
        (
            jnp.sum(grad_second_inner * second_normed, axis=(0, 1)),
            jnp.sum(grad_second_inner, axis=(0, 1)),
            bias_point_local,
            bias_head_local,
        ),
        ("wide", "narrow"),
    )
    hidden_gradient = norm_back(
        grad_second_inner,
        second_normed,
        second_scale,
        second_gain,
        grad_second_gain,
        grad_second_shift,
        weight,
        counted,
    ).astype(jnp.bfloat16)
    padded_gradient = with_halo(hidden_gradient, (("narrow", 1),), DILATION_STEP)
    grad_first_active = jnp.einsum(
        "wbh,ch->wbc",
        padded_gradient[:, 2 * DILATION_STEP : 2 * DILATION_STEP + local_bin_count],
        convolution_kernel[0],
        preferred_element_type=jnp.float32,
    )
    for kernel_position in range(1, 3):
        start_offset = (2 - kernel_position) * DILATION_STEP
        grad_first_active = grad_first_active + jnp.einsum(
            "wbh,ch->wbc",
            padded_gradient[:, start_offset : start_offset + local_bin_count],
            convolution_kernel[kernel_position],
            preferred_element_type=jnp.float32,
        )
    grad_taps = [
        jnp.einsum(
            "wbc,wbh->ch",
            padded_input[
                :,
                kernel_position * DILATION_STEP : kernel_position * DILATION_STEP + local_bin_count,
            ],
            hidden_gradient,
            preferred_element_type=jnp.float32,
        )
        for kernel_position in range(3)
    ]
    grad_conv_local = jnp.concatenate(grad_taps, axis=0)
    grad_first_inner = gelu_back(first_inner, grad_first_active)
    grad_first_gain, grad_first_shift = lax.psum(
        (
            jnp.sum(grad_first_inner * first_normed, axis=(0, 1)),
            jnp.sum(grad_first_inner, axis=(0, 1)),
        ),
        ("wide", "narrow"),
    )
    grad_tokens = grad_summed + norm_back(
        grad_first_inner,
        first_normed,
        first_scale,
        first_gain,
        grad_first_gain,
        grad_first_shift,
        weight,
        counted,
    )
    grad_conv, grad_point = (
        lax.psum_scatter(grad_conv_local, ("wide", "narrow"), scatter_dimension=0, tiled=True),
        lax.psum_scatter(grad_point_local, ("wide", "narrow"), scatter_dimension=0, tiled=True),
    )
    return (
        block,
        tracks,
        grad_tokens,
        grad_conv,
        grad_point,
        grad_head,
        grad_first_gain,
        grad_first_shift,
        grad_second_gain,
        grad_second_shift,
        grad_point_bias,
        grad_head_bias,
    )


def solution(mesh):
    placed = (
        P("wide", "narrow", None),
        P("wide", "narrow"),
        P(("wide", "narrow"), None),
        P(("wide", "narrow"), None),
        P(("wide", "narrow"), None),
        P(),
        P(),
        P(),
        P(),
        P(),
        P(),
        P("wide", "narrow", None),
        P("wide", None, "narrow"),
    )
    return jax.shard_map(
        shards,
        mesh=mesh,
        in_specs=placed,
        out_specs=(
            P("wide", "narrow", None),
            P("wide", None, "narrow"),
            P("wide", "narrow", None),
            P(("wide", "narrow"), None),
            P(("wide", "narrow"), None),
            P(("wide", "narrow"), None),
            P(),
            P(),
            P(),
            P(),
            P(),
            P(),
        ),
        check_vma=False,
    )
```

profile of v0, /device:TPU:0, one launch (start us, length us, event | category | flops | bytes accessed | tf_op | source)
XLA Modules:
  0.0 800.7 jit_solution(4075093609060179027)
XLA Ops:
  10.8 3.0 fusion.36
  13.7 42.3 %all-reduce.4 = (f32[768]{0:T(1024)S(1)}, f32[]{:T(128)}) all-reduce(f32[768]{0:T(1024)S(1)} %fusion.36, f32[]{:T(128)} %convert_reduce_fusion.2), channel_id=1, replica_groups=mesh['wide'=8,'narrow'=4] {'wide','narrow'}, use_global_device_ids=true, to_apply=%region_1.0 | all-reduce | flops 769 | bytes 6152 | tf_op jit(solution)/shard_map/psum | solution.py:24
  56.7 2.9 fusion.38
  59.6 40.8 %psum.82 = f32[768]{0:T(1024)S(1)} all-reduce(f32[768]{0:T(1024)S(1)} %fusion.38), channel_id=1, replica_groups=mesh['wide'=8,'narrow'=4] {'wide','narrow'}, use_global_device_ids=true, to_apply=%region_5.0 | all-reduce | flops 768 | bytes 6144 | tf_op jit(solution)/shard_map/psum | solution.py:29
  101.1 5.4 fusion.24
  112.3 48.0 %all_gather.13 = bf16[768,384]{1,0:T(8,128)(2,1)S(1)} all-gather(bf16[24,384]{1,0:T(8,128)(2,1)S(1)} %copy-done.20), channel_id=1, replica_groups=mesh['wide'=8,'narrow'=4] {'wide','narrow'}, dimensions={0}, use_global_device_ids=true | all-gather | bytes 608256 | tf_op jit(solution)/shard_map/all_gather | solution.py:86
  160.3 4.7 fusion.60
  165.0 2.2 fusion.47
  167.3 4.1 multiply_reduce_fusion.1
  171.4 37.1 %psum.83 = f32[384]{0:T(512)S(1)} all-reduce(f32[384]{0:T(512)S(1)} %get-tuple-element.33), channel_id=1, replica_groups=mesh['wide'=8,'narrow'=4] {'wide','narrow'}, use_global_device_ids=true, to_apply=%region_7.0 | all-reduce | flops 384 | bytes 3072 | tf_op jit(solution)/shard_map/psum | solution.py:24
  209.2 2.7 fusion.46
  211.8 41.1 %psum.84 = f32[384]{0:T(512)S(1)} all-reduce(f32[384]{0:T(512)S(1)} %fusion.46), channel_id=1, replica_groups=mesh['wide'=8,'narrow'=4] {'wide','narrow'}, use_global_device_ids=true, to_apply=%region_9.0 | all-reduce | flops 384 | bytes 3072 | tf_op jit(solution)/shard_map/psum | solution.py:29
  253.7 8.8 %fusion.37 = bf16[10,256,768]{2,1,0:T(8,128)(2,1)} fusion(bf16[10,256,768]{2,1,0:T(8,128)(2,1)} %param.13, f32[768]{0:T(1024)S(1)} %copy-done.34, bf16[768,384]{1,0:T(8,128)(2,1)S(1)} %all_gather.13, f32[10,256,384]{2,1,0:T(8,128)} %get-tuple-element.34, f32[384]{0:T(512)S(1)} %copy-done.35, f32[384]{0:T(512)S(1)} %copy-done.21, ...), kind=kOutput, calls=%fused_computation.49 | convolution fusion | flops 1530593280 | bytes 12395520 | tf_op jit(solution)/shard_map/wbh,ch->wbc/dot_general | solution.py:100
  262.5 73.0 %convert_reduce_fusion = (f32[5313]{0:T(1024)S(1)}, bf16[10,5313,256]{2,1,0:T(8,128)(2,1)}, bf16[10,5313,256]{2,1,0:T(8,128)(2,1)}) fusion(f32[5313]{0:T(1024)S(1)} %copy-done.33, f32[10,256]{1,0:T(8,128)S(1)} %convert_element_type.42, bf16[10,5313,256]{2,1,0:T(8,128)(2,1)} %param.25, bf16[10,256,768]{2,1,0:T(8,128)(2,1)} %fusion.37, ...), kind=kOutput, calls=%fused_computation.13 | convolution fusion | flops 21122775040 | bytes 93753352 | tf_op jit(solution)/shard_map/wbc,ct->wtb/dot_general | solution.py:105
  335.6 41.4 %convert_reduce_fusion.1 = (f32[768]{0:T(1024)S(1)}, bf16[10,256,768]{2,1,0:T(8,128)(2,1)S(1)}, f32[10,256,768]{2,1,0:T(8,128)}) fusion(f32[10,256]{1,0:T(8,128)S(1)} %convert_element_type.42, bf16[10,256,768]{2,1,0:T(8,128)(2,1)} %param.24, bf16[10,5313,256]{2,1,0:T(8,128)(2,1)} %get-tuple-element.25, bf16[768,5313]{1,0:T(8,128)(2,1)} %all-gather.5.cloned.1.call-done), kind=kOutput, calls=%fused_computation.51 | convolution fusion | flops 20903362560 | bytes 51105280 | tf_op jit(solution)/shard_map/wtb,ct->wbc/dot_general | solution.py:116
  379.0 3.4 convolution_bitcast_fusion.1
  382.4 8.9 %fusion.68 = (f32[384]{0:T(512)S(1)}, f32[384]{0:T(512)S(1)}, f32[10,256,384]{2,1,0:T(8,128)}) fusion(f32[384]{0:T(512)S(1)} %copy-done.24, f32[10,256,384]{2,1,0:T(8,128)} %get-tuple-element.34, f32[384]{0:T(512)S(1)} %copy-done.19, f32[384]{0:T(512)S(1)} %copy-done.36, f32[384]{0:T(512)S(1)} %copy-done.22, bf16[10,256,768]{2,1,0:T(8,128)(2,1)} %copy-done.37, ...), kind=kOutput, calls=%fused_computation.108 | convolution fusion | flops 1535507712 | bytes 12395520 | tf_op jit(solution)/shard_map/ldo,ov->ldv/dot_general | solution.py:145
  391.3 39.6 %all-reduce.3 = (f32[384]{0:T(512)S(1)}, f32[384]{0:T(512)S(1)}) all-reduce(f32[384]{0:T(512)S(1)} %get-tuple-element.15, f32[384]{0:T(512)S(1)} %get-tuple-element.14), channel_id=1, replica_groups=mesh['wide'=8,'narrow'=4] {'wide','narrow'}, use_global_device_ids=true, to_apply=%region_13.14 | all-reduce | flops 768 | bytes 6144 | tf_op jit(solution)/shard_map/psum | solution.py:151
  430.9 4.1 multiply_convert_fusion
  435.4 2.2 fusion.55
  437.6 2.3 fusion.56
  439.9 2.2 convolution_bitcast_fusion.2
  442.1 2.1 pad_maximum_fusion.2
  444.3 29.4 %convolution_bitcast_fusion = f32[768,5313]{1,0:T(8,128)} fusion(bf16[10,256,768]{2,1,0:T(8,128)(2,1)} %fusion.37, bf16[10,5313,256]{2,1,0:T(8,128)(2,1)} %get-tuple-element.25), kind=kOutput, calls=%fused_computation.19 | convolution fusion | flops 20891566080 | bytes 47456256 | tf_op jit(solution)/shard_map/wbc,wtb->ct/dot_general | solution.py:124
  475.1 3.0 collective-permute-start.3
  478.1 3.3 fusion.59
  481.5 3.5 fusion.53
  485.0 11.6 %fusion.67 = (f32[768]{0:T(1024)S(1)}, f32[768]{0:T(1024)S(1)}, f32[10,256,768]{2,1,0:T(8,128)}) fusion(f32[768]{0:T(1024)S(1)} %copy-done.17, f32[768]{0:T(1024)S(1)} %copy-done.13, bf16[10,256,768]{2,1,0:T(8,128)(2,1)S(1)} %copy-done, f32[768]{0:T(1024)S(1)} %copy-done.26, f32[768]{0:T(1024)S(1)} %copy-done.15, ...), kind=kOutput, calls=%fused_computation.107 | convolution fusion | flops 1570896384 | bytes 30183936 | tf_op jit(solution)/shard_map/wbh,ch->wbc/dot_general | solution.py:179
  496.6 41.1 %all-reduce.2 = (f32[768]{0:T(1024)S(1)}, f32[768]{0:T(1024)S(1)}, f32[768]{0:T(1024)}, f32[5313]{0:T(1024)}) all-reduce(f32[768]{0:T(1024)S(1)} %get-tuple-element.13, f32[768]{0:T(1024)S(1)} %get-tuple-element.12, f32[768]{0:T(1024)S(1)} %get-tuple-element.26, ...), channel_id=1, replica_groups=mesh['wide'=8,'narrow'=4] {'wide','narrow'}, use_global_device_ids=true, to_apply=%region_17.18 | all-reduce | flops 7617 | bytes 60936 | tf_op jit(solution)/shard_map/psum | solution.py:199
  537.7 13.5 %fusion.31 = f32[10,256,768]{2,1,0:T(8,128)} fusion(bf16[10,256,768]{2,1,0:T(8,128)(2,1)} %param.13, f32[10,256,768]{2,1,0:T(8,128)} %get-tuple-element.37, f32[10,256,768]{2,1,0:T(8,128)} %get-tuple-element.35, bf16[10,256,768]{2,1,0:T(8,128)(2,1)} %param.24, f32[768]{0:T(1024)S(1)} %get-tuple-element.16, f32[768]{0:T(1024)S(1)} %mul.333, ...), kind=kLoop, calls=%fused_computation.43 | loop fusion | flops 27525120 | bytes 31493120 | tf_op jit(solution)/shard_map/add | solution.py:206
  551.3 45.8 %reduce-scatter.10.cloned.1.call-done = f32[72,384]{1,0:T(8,128)} async-done(((f32[2304,384]{1,0:T(8,128)}), f32[72,384]{1,0:T(8,128)}) %reduce-scatter.10.cloned.1.call-update) | async-done | bytes 110608
  597.0 196.7 %reduce-scatter.8.cloned.1.call-done = f32[24,5313]{1,0:T(8,128)} async-done(((f32[768,5313]{1,0:T(8,128)}), f32[24,5313]{1,0:T(8,128)}) %reduce-scatter.8.cloned.1.call-update) | async-done | bytes 510064 | tf_op jit(solution)/shard_map/reduce_scatter | solution.py:123
  (107 shorter events, 15.8 us)
Async XLA Ops:
  7.2 153.1 %all-gather.3.cloned.1.call-start = ((), (), s32[]{:S(2)}) async-start(), calls=%async_computation.3 | async-start | bytes 1824768 | tf_op jit(solution)/shard_map/all_gather | solution.py:85
  7.9 254.6 %all-gather.5.cloned.1.call-start = ((), (), s32[]{:S(2)}) async-start(), calls=%async_computation.4 | async-start | bytes 8515584 | tf_op jit(solution)/shard_map/all_gather | solution.py:108
  8.7 542.6 %reduce-scatter.12.cloned.1.call-start = ((), (), s32[]{:S(2)}) async-start(), calls=%async_computation.7 | async-start | bytes 1216512
  10.8 90.3 %copy-start.14 = (f32[768]{0:T(1024)S(1)}, f32[768]{0:T(1024)}, u32[]{:S(2)}) copy-start(f32[768]{0:T(1024)} %param.18) | copy-start | bytes 9220
  10.8 90.3 %copy-start.25 = (f32[768]{0:T(1024)S(1)}, f32[768]{0:T(1024)}, u32[]{:S(2)}) copy-start(f32[768]{0:T(1024)} %param.19) | copy-start | bytes 9220
  56.7 49.8 %copy-start.12 = (f32[768]{0:T(1024)}, f32[768]{0:T(1024)S(1)}, u32[]{:S(2)}) copy-start(f32[768]{0:T(1024)S(1)} %broadcast_divide_fusion.1) | copy-start | bytes 9220
  101.0 5.4 copy-start.16
  101.1 10.0 %copy-start.11 = (s32[10,256]{1,0:T(8,128)S(1)}, s32[10,256]{1,0:T(8,128)}, u32[]{:S(2)}) copy-start(s32[10,256]{1,0:T(8,128)} %param.14) | copy-start | bytes 30724
  101.1 11.2 %copy-start.20 = (bf16[24,384]{1,0:T(8,128)(2,1)S(1)}, bf16[24,384]{1,0:T(8,128)(2,1)}, u32[]{:S(2)}) copy-start(bf16[24,384]{1,0:T(8,128)(2,1)} %param.16) | copy-start | bytes 55300
  108.4 56.6 %collective-permute-start = (bf16[10,11,768]{2,1,0:T(8,128)(2,1)S(1)}, bf16[10,11,768]{2,1,0:T(8,128)(2,1)S(1)}, u32[]{:S(2)}, u32[]{:S(2)}) collective-permute-start(bf16[10,11,768]{2,1,0:T(8,128)(2,1)S(1)} %get-tuple-element.30), channel_id=1, source_target_pairs={{0,1},{1,2},{2,3},{4,5},{5,6},{6,7},{8,9},{9,10},{10,11},{12,13},{... | collective-permute-start | bytes 506888 | tf_op jit(solution)/shard_map/ppermute | solution.py:17
  109.7 57.5 %collective-permute-start.1 = (bf16[10,11,768]{2,1,0:T(8,128)(2,1)S(1)}, bf16[10,11,768]{2,1,0:T(8,128)(2,1)S(1)}, u32[]{:S(2)}, u32[]{:S(2)}) collective-permute-start(bf16[10,11,768]{2,1,0:T(8,128)(2,1)S(1)} %get-tuple-element.29), channel_id=1, source_target_pairs={{1,0},{2,1},{3,2},{5,4},{6,5},{7,6},{9,8},{10,9},{11,10},{13,12},{... | collective-permute-start | bytes 506888 | tf_op jit(solution)/shard_map/ppermute | solution.py:18
  160.3 93.4 %copy-start.6 = (bf16[768,384]{1,0:T(8,128)(2,1)}, bf16[768,384]{1,0:T(8,128)(2,1)S(1)}, u32[]{:S(2)}) copy-start(bf16[768,384]{1,0:T(8,128)(2,1)S(1)} %all_gather.13) | copy-start | bytes 1769476
  160.3 4.7 copy-start.2
  160.3 4.7 copy-start.5
  171.4 82.3 %copy-start.21 = (f32[384]{0:T(512)S(1)}, f32[384]{0:T(512)}, u32[]{:S(2)}) copy-start(f32[384]{0:T(512)} %param.20) | copy-start | bytes 4612
  171.4 82.3 %copy-start.34 = (f32[768]{0:T(1024)S(1)}, f32[768]{0:T(1024)}, u32[]{:S(2)}) copy-start(f32[768]{0:T(1024)} %param.22) | copy-start | bytes 9220
  171.4 82.3 %copy-start.35 = (f32[384]{0:T(512)S(1)}, f32[384]{0:T(512)}, u32[]{:S(2)}) copy-start(f32[384]{0:T(512)} %param.21) | copy-start | bytes 4612
  209.2 53.4 %copy-start.18 = (f32[384]{0:T(512)}, f32[384]{0:T(512)S(1)}, u32[]{:S(2)}) copy-start(f32[384]{0:T(512)S(1)} %broadcast_divide_fusion.2) | copy-start | bytes 4612
  253.7 8.8 %copy-start.23 = (f32[384]{0:T(512)}, f32[384]{0:T(512)S(1)}, u32[]{:S(2)}) copy-start(f32[384]{0:T(512)S(1)} %add_rsqrt_fusion.1) | copy-start | bytes 4612
  253.7 8.8 %copy-start.33 = (f32[5313]{0:T(1024)S(1)}, f32[5313]{0:T(1024)}, u32[]{:S(2)}) copy-start(f32[5313]{0:T(1024)} %param.23) | copy-start | bytes 63760
  335.5 43.4 %copy-start.4 = (f32[10,256,384]{2,1,0:T(8,128)S(1)}, f32[10,256,384]{2,1,0:T(8,128)}, u32[]{:S(2)}) copy-start(f32[10,256,384]{2,1,0:T(8,128)} %get-tuple-element.34) | copy-start | bytes 11796484
  335.6 43.4 %copy-start.19 = (f32[384]{0:T(512)S(1)}, f32[384]{0:T(512)}, u32[]{:S(2)}) copy-start(f32[384]{0:T(512)} %copy-done.18) | copy-start | bytes 4612
  335.6 43.4 %copy-start.22 = (f32[384]{0:T(512)S(1)}, f32[384]{0:T(512)}, u32[]{:S(2)}) copy-start(f32[384]{0:T(512)} %param.20) | copy-start | bytes 4612
  335.6 43.4 %copy-start.24 = (f32[384]{0:T(512)S(1)}, f32[384]{0:T(512)}, u32[]{:S(2)}) copy-start(f32[384]{0:T(512)} %copy-done.23) | copy-start | bytes 4612
  335.6 43.4 %copy-start.36 = (f32[384]{0:T(512)S(1)}, f32[384]{0:T(512)}, u32[]{:S(2)}) copy-start(f32[384]{0:T(512)} %param.21) | copy-start | bytes 4612
  382.4 48.5 %copy-start.10 = (f32[10,256]{1,0:T(8,128)S(1)}, f32[10,256]{1,0:T(8,128)}, u32[]{:S(2)}) copy-start(f32[10,256]{1,0:T(8,128)} %broadcast_divide_fusion) | copy-start | bytes 30724
  391.3 205.8 %reduce-scatter.10.cloned.1.call-start = ((), (), s32[]{:S(2)}) async-start(), calls=%async_computation.6 | async-start | bytes 3649536
  444.2 349.5 %reduce-scatter.8.cloned.1.call-start = ((), (), s32[]{:S(2)}) async-start(), calls=%async_computation.5 | async-start | bytes 17031168 | tf_op jit(solution)/shard_map/reduce_scatter | solution.py:123
  473.8 7.7 collective-permute-start.2
  475.1 9.9 %collective-permute-start.3 = (bf16[10,11,384]{2,1,0:T(8,128)(2,1)S(1)}, bf16[10,11,384]{2,1,0:T(8,128)(2,1)S(1)}, u32[]{:S(2)}, u32[]{:S(2)}) collective-permute-start(bf16[10,11,384]{2,1,0:T(8,128)(2,1)S(1)} %get-tuple-element.31), channel_id=1, source_target_pairs={{0,1},{1,2},{2,3},{4,5},{5,6},{6,7},{8,9},{9,10},{10,11},{12,13},{... | collective-permute-start | bytes 253448 | tf_op jit(solution)/shard_map/ppermute | solution.py:17
  537.7 13.5 %copy-start.27 = (f32[768]{0:T(1024)}, f32[768]{0:T(1024)S(1)}, u32[]{:S(2)}) copy-start(f32[768]{0:T(1024)S(1)} %get-tuple-element.16) | copy-start | bytes 9220
  537.7 13.5 %copy-start.28 = (f32[768]{0:T(1024)}, f32[768]{0:T(1024)S(1)}, u32[]{:S(2)}) copy-start(f32[768]{0:T(1024)S(1)} %get-tuple-element.17) | copy-start | bytes 9220
  (15 other events, 50.8 us)
Sparse Core Ops, SparseCore 0:
  10.8 58.2 all-gather.2
  72.0 79.8 all-gather.4
  391.4 97.2 reduce-scatter.11
  494.6 102.4 reduce-scatter.9
  603.8 189.8 reduce-scatter.7
where the time goes:
time: 810 us; the launch traced here: 801 us
  blocking collectives  290 us (36%)
  waiting for transfers between devices  244 us (30%)
  matrix products  201 us (25%)
  other arithmetic  39.6 us (5%)
  between operations  14.8 us (2%)
    reduce_scatter x1, waiting for transfers between devices, shards(): lax.psum_scatter(jnp.einsum('wbc,wtb->ct', window_part, grad_logits, pref...  197 us
    psum x2, blocking collectives, norm_stats(): lax.psum(jnp.sum(weight * centred * centred, axis=(0, 1)), ('wide', 'narr...  81.9 us
    psum x2, blocking collectives, norm_stats(): lax.psum((jnp.sum(values * weight, axis=(0, 1)), jnp.sum(weight)), ('wide...  79.4 us
    dot_general x1, matrix products, shards(): jnp.einsum('wbc,ct->wtb', window_part, lax.all_gather(head_weight, ('wide...  73 us
    all_gather x1, blocking collectives, shards(): lax.all_gather(point_weight, ('wide', 'narrow'), axis=0, tiled=True)  48 us
    unnamed x7, waiting for transfers between devices  47.2 us
    dot_general x1, matrix products, shards(): jnp.einsum('wtb,ct->wbc', grad_logits, lax.all_gather(head_weight, ('wide...  41.4 us
    psum x1, blocking collectives, shards(): lax.psum((jnp.sum(grad_first_inner * first_normed, axis=(0, 1)), jnp.sum(...  41.1 us
  transfers between devices with their start and end apart: 9, of which 2 were waited for; matrix products, arithmetic and copies ran while one was open for 14% of the time, Pallas kernels for 0%

commit v1 on v0

--- a/solution.py
+++ b/solution.py
@@ -5,6 +5,18 @@
 
 DILATION_STEP = 11
 epsilon = 1e-05
+
+
+def collect(shard, axis, dim):
+    ways, here = (lax.axis_size(axis), lax.axis_index(axis))
+    grown, reach = (shard, 1)
+    while reach < ways:
+        theirs = lax.ppermute(grown, axis, [(d, d ^ reach) for d in range(ways)])
+        mine_first = jnp.concatenate([grown, theirs], axis=dim)
+        theirs_first = jnp.concatenate([theirs, grown], axis=dim)
+        grown = jnp.where(here & reach == 0, mine_first, theirs_first)
+        reach = 2 * reach
+    return grown
 
 
 def with_halo(shard, sides, width):
@@ -83,7 +95,7 @@
     source = tokens.astype(jnp.float32)
     conv_full, point_full = (
         lax.all_gather(conv_weight, ("wide", "narrow"), axis=0, tiled=True),
-        lax.all_gather(point_weight, ("wide", "narrow"), axis=0, tiled=True),
+        collect(point_weight, ("wide", "narrow"), 0),
     )
     first_mean, first_scale, counted = norm_stats(source, weight)
     first_normed = (source - first_mean) * first_scale

time: 810 us -> 797 us (0.984)
  matrix products: 201 us -> 190 us
    dot_general x1, matrix products: 41.4 us -> 30.2 us  [shards(): jnp.einsum('wtb,ct->wbc', grad_logits, lax.all_gather(head_weight, ('wide...]
  transfers between devices with their start and end apart: 9 -> 14, of which waited for: 2 -> 3; matrix products, arithmetic and copies ran while one was open for 14% -> 16% of each run, Pallas kernels for 0% -> 0%
where the time goes in v1:
time: 797 us; the launch traced here: 791 us
  blocking collectives  288 us (36%)
  waiting for transfers between devices  241 us (30%)
  matrix products  190 us (24%)
  other arithmetic  40.6 us (5%)
  between operations  14.9 us (2%)
  starting transfers between devices  12 us (2%)
    reduce_scatter x1, waiting for transfers between devices, shards(): lax.psum_scatter(jnp.einsum('wbc,wtb->ct', window_part, grad_logits, pref...  197 us
    psum x2, blocking collectives, norm_stats(): lax.psum((jnp.sum(values * weight, axis=(0, 1)), jnp.sum(weight)), ('wide...  81.5 us
    psum x2, blocking collectives, norm_stats(): lax.psum(jnp.sum(weight * centred * centred, axis=(0, 1)), ('wide', 'narr...  79 us
    dot_general x1, matrix products, shards(): jnp.einsum('wbc,ct->wtb', window_part, lax.all_gather(head_weight, ('wide...  73.5 us
    all_gather x1, blocking collectives, shards(): lax.all_gather(point_weight, ('wide', 'narrow'), axis=0, tiled=True)  47.1 us
    psum x1, blocking collectives, shards(): lax.psum((jnp.sum(grad_second_inner * second_normed, axis=(0, 1)), jnp.su...  41.4 us
    unnamed x7, waiting for transfers between devices  39.8 us
    psum x1, blocking collectives, shards(): lax.psum((jnp.sum(grad_first_inner * first_normed, axis=(0, 1)), jnp.sum(...  39.3 us
  transfers between devices with their start and end apart: 14, of which 3 were waited for; matrix products, arithmetic and copies ran while one was open for 16% of the time, Pallas kernels for 0%

profile of v1, /device:TPU:0, one launch (start us, length us, event | category | flops | bytes accessed | tf_op | source)
XLA Modules:
  0.0 791.2 jit_solution(15318703242336893383)
XLA Ops:
  11.3 3.0 fusion.36
  14.3 41.8 %all-reduce.4 = (f32[768]{0:T(1024)S(1)}, f32[]{:T(128)}) all-reduce(f32[768]{0:T(1024)S(1)} %fusion.36, f32[]{:T(128)} %convert_reduce_fusion.2), channel_id=1, replica_groups=mesh['wide'=8,'narrow'=4] {'wide','narrow'}, use_global_device_ids=true, to_apply=%region_1.2 | all-reduce | flops 769 | bytes 6152 | tf_op jit(solution)/shard_map/psum | solution.py:36
  56.7 2.9 fusion.38
  59.6 40.6 %psum.82 = f32[768]{0:T(1024)S(1)} all-reduce(f32[768]{0:T(1024)S(1)} %fusion.38), channel_id=1, replica_groups=mesh['wide'=8,'narrow'=4] {'wide','narrow'}, use_global_device_ids=true, to_apply=%region_5.6 | all-reduce | flops 768 | bytes 6144 | tf_op jit(solution)/shard_map/psum | solution.py:41
  101.0 6.7 fusion.24
  107.7 2.5 collective-permute-start.3
  115.7 47.1 %all_gather.13 = bf16[768,384]{1,0:T(8,128)(2,1)} all-gather(bf16[24,384]{1,0:T(8,128)(2,1)S(1)} %copy-done.10), channel_id=1, replica_groups=mesh['wide'=8,'narrow'=4] {'wide','narrow'}, dimensions={0}, use_global_device_ids=true | all-gather | bytes 608256 | tf_op jit(solution)/shard_map/all_gather | solution.py:145
  164.2 4.8 collective-permute-done.5
  169.2 4.6 fusion.67
  176.1 4.1 multiply_reduce_fusion.1
  180.2 39.7 %psum.83 = f32[384]{0:T(512)S(1)} all-reduce(f32[384]{0:T(512)S(1)} %get-tuple-element.33), channel_id=1, replica_groups=mesh['wide'=8,'narrow'=4] {'wide','narrow'}, use_global_device_ids=true, to_apply=%region_7.8 | all-reduce | flops 384 | bytes 3072 | tf_op jit(solution)/shard_map/psum | solution.py:36
  220.6 2.7 fusion.46
  223.3 38.4 %psum.84 = f32[384]{0:T(512)S(1)} all-reduce(f32[384]{0:T(512)S(1)} %fusion.46), channel_id=1, replica_groups=mesh['wide'=8,'narrow'=4] {'wide','narrow'}, use_global_device_ids=true, to_apply=%region_9.10 | all-reduce | flops 384 | bytes 3072 | tf_op jit(solution)/shard_map/psum | solution.py:41
  262.5 8.9 %fusion.37 = bf16[10,256,768]{2,1,0:T(8,128)(2,1)} fusion(bf16[10,256,768]{2,1,0:T(8,128)(2,1)} %param.13, f32[768]{0:T(1024)S(1)} %copy-done.32, bf16[384,384]{1,0:T(8,128)(2,1)S(1)} %collective-permute-done.6, bf16[384,384]{1,0:T(8,128)(2,1)S(1)} %maximum_select_fusion.1, pred[]{:T(512)S(6)} %eq.15, f32[10,256,384]{2,1,0:T(8,128)} %get-tuple-element.34, ...), kind=kOutput, calls=%fused_computation.49 | convolution fusion | flops 1533247488 | bytes 12395521 | tf_op jit(solution)/shard_map/wbh,ch->wbc/dot_general | solution.py:112
  271.4 73.5 %convert_reduce_fusion = (f32[5313]{0:T(1024)S(1)}, bf16[10,5313,256]{2,1,0:T(8,128)(2,1)}, bf16[10,5313,256]{2,1,0:T(8,128)(2,1)}) fusion(f32[5313]{0:T(1024)S(1)} %copy-done.31, f32[10,256]{1,0:T(8,128)S(1)} %convert_element_type.42, bf16[10,5313,256]{2,1,0:T(8,128)(2,1)} %param.25, bf16[10,256,768]{2,1,0:T(8,128)(2,1)} %fusion.37, ...), kind=kOutput, calls=%fused_computation.13 | convolution fusion | flops 21122775040 | bytes 93753352 | tf_op jit(solution)/shard_map/wbc,ct->wtb/dot_general | solution.py:117
  344.9 30.2 %convert_reduce_fusion.1 = (f32[768]{0:T(1024)S(1)}, bf16[10,256,768]{2,1,0:T(8,128)(2,1)S(1)}, f32[10,256,768]{2,1,0:T(8,128)}) fusion(f32[10,256]{1,0:T(8,128)S(1)} %convert_element_type.42, bf16[10,256,768]{2,1,0:T(8,128)(2,1)} %param.24, bf16[10,5313,256]{2,1,0:T(8,128)(2,1)} %get-tuple-element.25, bf16[768,5313]{1,0:T(8,128)(2,1)} %all-gather.5.cloned.1.call-done), kind=kOutput, calls=%fused_computation.51 | convolution fusion | flops 20903362560 | bytes 51105280 | tf_op jit(solution)/shard_map/wtb,ct->wbc/dot_general | solution.py:128
  377.1 3.4 convolution_bitcast_fusion.1
  380.6 8.9 %fusion.76 = (f32[384]{0:T(512)S(1)}, f32[384]{0:T(512)S(1)}, f32[10,256,384]{2,1,0:T(8,128)}) fusion(f32[384]{0:T(512)S(1)} %copy-done.22, f32[10,256,384]{2,1,0:T(8,128)} %get-tuple-element.34, f32[384]{0:T(512)S(1)} %copy-done.18, f32[384]{0:T(512)S(1)} %copy-done.34, f32[384]{0:T(512)S(1)} %copy-done.20, bf16[10,256,768]{2,1,0:T(8,128)(2,1)} %copy-done.35, ...), kind=kOutput, calls=%fused_computation.120 | convolution fusion | flops 1535507712 | bytes 12395520 | tf_op jit(solution)/shard_map/ldo,ov->ldv/dot_general | solution.py:157
  389.5 41.4 %all-reduce.3 = (f32[384]{0:T(512)S(1)}, f32[384]{0:T(512)S(1)}) all-reduce(f32[384]{0:T(512)S(1)} %get-tuple-element.15, f32[384]{0:T(512)S(1)} %get-tuple-element.14), channel_id=1, replica_groups=mesh['wide'=8,'narrow'=4] {'wide','narrow'}, use_global_device_ids=true, to_apply=%region_13.14 | all-reduce | flops 768 | bytes 6144 | tf_op jit(solution)/shard_map/psum | solution.py:163
  431.0 4.1 multiply_convert_fusion
  435.4 2.2 fusion.55
  437.7 2.3 fusion.56
  439.9 2.2 convolution_bitcast_fusion.2
  444.3 29.5 %convolution_bitcast_fusion = f32[768,5313]{1,0:T(8,128)} fusion(bf16[10,256,768]{2,1,0:T(8,128)(2,1)} %fusion.37, bf16[10,5313,256]{2,1,0:T(8,128)(2,1)} %get-tuple-element.25), kind=kOutput, calls=%fused_computation.19 | convolution fusion | flops 20891566080 | bytes 47456256 | tf_op jit(solution)/shard_map/wbc,wtb->ct/dot_general | solution.py:136
  475.2 3.0 collective-permute-start.8
  478.2 3.3 fusion.66
  481.6 3.5 fusion.53
  485.1 11.6 %fusion.75 = (f32[768]{0:T(1024)S(1)}, f32[768]{0:T(1024)S(1)}, f32[10,256,768]{2,1,0:T(8,128)}) fusion(f32[768]{0:T(1024)S(1)} %copy-done.16, f32[768]{0:T(1024)S(1)} %copy-done.12, bf16[10,256,768]{2,1,0:T(8,128)(2,1)S(1)} %copy-done, f32[768]{0:T(1024)S(1)} %copy-done.24, f32[768]{0:T(1024)S(1)} %copy-done.14, ...), kind=kOutput, calls=%fused_computation.119 | convolution fusion | flops 1570896384 | bytes 30183936 | tf_op jit(solution)/shard_map/wbh,ch->wbc/dot_general | solution.py:191
  496.7 39.3 %all-reduce.2 = (f32[768]{0:T(1024)S(1)}, f32[768]{0:T(1024)S(1)}, f32[768]{0:T(1024)}, f32[5313]{0:T(1024)}) all-reduce(f32[768]{0:T(1024)S(1)} %get-tuple-element.13, f32[768]{0:T(1024)S(1)} %get-tuple-element.12, f32[768]{0:T(1024)S(1)} %get-tuple-element.26, ...), channel_id=1, replica_groups=mesh['wide'=8,'narrow'=4] {'wide','narrow'}, use_global_device_ids=true, to_apply=%region_17.18 | all-reduce | flops 7617 | bytes 60936 | tf_op jit(solution)/shard_map/psum | solution.py:211
  536.0 13.1 %fusion.31 = f32[10,256,768]{2,1,0:T(8,128)} fusion(bf16[10,256,768]{2,1,0:T(8,128)(2,1)} %param.13, f32[10,256,768]{2,1,0:T(8,128)} %get-tuple-element.37, f32[10,256,768]{2,1,0:T(8,128)} %get-tuple-element.35, bf16[10,256,768]{2,1,0:T(8,128)(2,1)} %param.24, f32[768]{0:T(1024)S(1)} %get-tuple-element.16, f32[768]{0:T(1024)S(1)} %mul.337, ...), kind=kLoop, calls=%fused_computation.43 | loop fusion | flops 27525120 | bytes 31493120 | tf_op jit(solution)/shard_map/add | solution.py:218
  549.2 38.4 %reduce-scatter.10.cloned.1.call-done = f32[72,384]{1,0:T(8,128)} async-done(((f32[2304,384]{1,0:T(8,128)}), f32[72,384]{1,0:T(8,128)}) %reduce-scatter.10.cloned.1.call-update) | async-done | bytes 110608
  587.5 196.6 %reduce-scatter.8.cloned.1.call-done = f32[24,5313]{1,0:T(8,128)} async-done(((f32[768,5313]{1,0:T(8,128)}), f32[24,5313]{1,0:T(8,128)}) %reduce-scatter.8.cloned.1.call-update) | async-done | bytes 510064 | tf_op jit(solution)/shard_map/reduce_scatter | solution.py:135
  (117 shorter events, 21.9 us)
Async XLA Ops:
  7.2 162.0 %all-gather.3.cloned.1.call-start = ((), (), s32[]{:S(2)}) async-start(), calls=%async_computation.3 | async-start | bytes 1824768 | tf_op jit(solution)/shard_map/all_gather | solution.py:97
  7.9 263.5 %all-gather.5.cloned.1.call-start = ((), (), s32[]{:S(2)}) async-start(), calls=%async_computation.4 | async-start | bytes 8515584 | tf_op jit(solution)/shard_map/all_gather | solution.py:120
  8.7 540.5 %reduce-scatter.12.cloned.1.call-start = ((), (), s32[]{:S(2)}) async-start(), calls=%async_computation.7 | async-start | bytes 1216512
  8.7 99.0 %collective-permute-start.2 = (bf16[24,384]{1,0:T(8,128)(2,1)}, bf16[24,384]{1,0:T(8,128)(2,1)S(1)}, u32[]{:S(2)}, u32[]{:S(2)}) collective-permute-start(bf16[24,384]{1,0:T(8,128)(2,1)} %param.16), channel_id=1, source_target_pairs={{0,1},{1,0},{2,3},{3,2},{4,5},{5,4},{6,7},{7,6},{8,9},{9,8},{10,11... | collective-permute-start | bytes 55304 | tf_op jit(solution)/shard_map/ppermute | solution.py:14
  11.3 89.6 %copy-start.13 = (f32[768]{0:T(1024)S(1)}, f32[768]{0:T(1024)}, u32[]{:S(2)}) copy-start(f32[768]{0:T(1024)} %param.18) | copy-start | bytes 9220
  11.3 89.6 %copy-start.23 = (f32[768]{0:T(1024)S(1)}, f32[768]{0:T(1024)}, u32[]{:S(2)}) copy-start(f32[768]{0:T(1024)} %param.19) | copy-start | bytes 9220
  56.7 51.0 %copy-start.11 = (f32[768]{0:T(1024)}, f32[768]{0:T(1024)S(1)}, u32[]{:S(2)}) copy-start(f32[768]{0:T(1024)S(1)} %broadcast_divide_fusion.1) | copy-start | bytes 9220
  101.0 62.0 %copy-start.9 = (s32[10,256]{1,0:T(8,128)S(1)}, s32[10,256]{1,0:T(8,128)}, u32[]{:S(2)}) copy-start(s32[10,256]{1,0:T(8,128)} %param.14) | copy-start | bytes 30724
  107.7 6.3 collective-permute-start.3
  111.4 62.5 %collective-permute-start = (bf16[10,11,768]{2,1,0:T(8,128)(2,1)S(1)}, bf16[10,11,768]{2,1,0:T(8,128)(2,1)S(1)}, u32[]{:S(2)}, u32[]{:S(2)}) collective-permute-start(bf16[10,11,768]{2,1,0:T(8,128)(2,1)S(1)} %get-tuple-element.30), channel_id=1, source_target_pairs={{0,1},{1,2},{2,3},{4,5},{5,6},{6,7},{8,9},{9,10},{10,11},{12,13},{... | collective-permute-start | bytes 506888 | tf_op jit(solution)/shard_map/ppermute | solution.py:29
  112.7 63.4 %collective-permute-start.1 = (bf16[10,11,768]{2,1,0:T(8,128)(2,1)S(1)}, bf16[10,11,768]{2,1,0:T(8,128)(2,1)S(1)}, u32[]{:S(2)}, u32[]{:S(2)}) collective-permute-start(bf16[10,11,768]{2,1,0:T(8,128)(2,1)S(1)} %get-tuple-element.29), channel_id=1, source_target_pairs={{1,0},{2,1},{3,2},{5,4},{6,5},{7,6},{9,8},{10,9},{11,10},{13,12},{... | collective-permute-start | bytes 506888 | tf_op jit(solution)/shard_map/ppermute | solution.py:30
  114.0 48.8 %collective-permute-start.4 = (bf16[96,384]{1,0:T(8,128)(2,1)S(1)}, bf16[96,384]{1,0:T(8,128)(2,1)S(1)}, u32[]{:S(2)}, u32[]{:S(2)}) collective-permute-start(bf16[96,384]{1,0:T(8,128)(2,1)S(1)} %maximum_select_fusion.3), channel_id=1, source_target_pairs={{0,4},{1,5},{2,6},{3,7},{4,0},{5,1},{6,2},{7,3},{8,12},{9,13},{10,... | collective-permute-start | bytes 221192 | tf_op jit(solution)/shard_map/ppermute | solution.py:14
  162.8 6.2 collective-permute-start.5
  169.1 93.3 %collective-permute-start.6 = (bf16[384,384]{1,0:T(8,128)(2,1)S(1)}, bf16[384,384]{1,0:T(8,128)(2,1)S(1)}, u32[]{:S(2)}, u32[]{:S(2)}) collective-permute-start(bf16[384,384]{1,0:T(8,128)(2,1)S(1)} %maximum_select_fusion.1), channel_id=1, source_target_pairs={{0,16},{1,17},{2,18},{3,19},{4,20},{5,21},{6,22},{7,23},{8,24},{9,... | collective-permute-start | bytes 884744 | tf_op jit(solution)/shard_map/ppermute | solution.py:14
  180.2 82.2 %copy-start.19 = (f32[384]{0:T(512)S(1)}, f32[384]{0:T(512)}, u32[]{:S(2)}) copy-start(f32[384]{0:T(512)} %param.20) | copy-start | bytes 4612
  180.2 82.2 %copy-start.32 = (f32[768]{0:T(1024)S(1)}, f32[768]{0:T(1024)}, u32[]{:S(2)}) copy-start(f32[768]{0:T(1024)} %param.22) | copy-start | bytes 9220
  180.2 82.2 %copy-start.33 = (f32[384]{0:T(512)S(1)}, f32[384]{0:T(512)}, u32[]{:S(2)}) copy-start(f32[384]{0:T(512)} %param.21) | copy-start | bytes 4612
  220.6 50.8 %copy-start.17 = (f32[384]{0:T(512)}, f32[384]{0:T(512)S(1)}, u32[]{:S(2)}) copy-start(f32[384]{0:T(512)S(1)} %broadcast_divide_fusion.2) | copy-start | bytes 4612
  262.4 9.0 %copy-start.21 = (f32[384]{0:T(512)}, f32[384]{0:T(512)S(1)}, u32[]{:S(2)}) copy-start(f32[384]{0:T(512)S(1)} %add_rsqrt_fusion.1) | copy-start | bytes 4612
  262.4 9.0 %copy-start.31 = (f32[5313]{0:T(1024)S(1)}, f32[5313]{0:T(1024)}, u32[]{:S(2)}) copy-start(f32[5313]{0:T(1024)} %param.23) | copy-start | bytes 63760
  344.9 32.2 %copy-start.3 = (f32[10,256,384]{2,1,0:T(8,128)S(1)}, f32[10,256,384]{2,1,0:T(8,128)}, u32[]{:S(2)}) copy-start(f32[10,256,384]{2,1,0:T(8,128)} %get-tuple-element.34) | copy-start | bytes 11796484
  344.9 32.2 %copy-start.18 = (f32[384]{0:T(512)S(1)}, f32[384]{0:T(512)}, u32[]{:S(2)}) copy-start(f32[384]{0:T(512)} %copy-done.17) | copy-start | bytes 4612
  344.9 32.2 %copy-start.20 = (f32[384]{0:T(512)S(1)}, f32[384]{0:T(512)}, u32[]{:S(2)}) copy-start(f32[384]{0:T(512)} %param.20) | copy-start | bytes 4612
  344.9 32.2 %copy-start.22 = (f32[384]{0:T(512)S(1)}, f32[384]{0:T(512)}, u32[]{:S(2)}) copy-start(f32[384]{0:T(512)} %copy-done.21) | copy-start | bytes 4612
  344.9 32.2 %copy-start.34 = (f32[384]{0:T(512)S(1)}, f32[384]{0:T(512)}, u32[]{:S(2)}) copy-start(f32[384]{0:T(512)} %param.21) | copy-start | bytes 4612
  380.6 50.4 %copy-start.8 = (f32[10,256]{1,0:T(8,128)S(1)}, f32[10,256]{1,0:T(8,128)}, u32[]{:S(2)}) copy-start(f32[10,256]{1,0:T(8,128)} %broadcast_divide_fusion) | copy-start | bytes 30724
  380.6 207.0 %reduce-scatter.10.cloned.1.call-start = ((), (), s32[]{:S(2)}) async-start(), calls=%async_computation.6 | async-start | bytes 3649536
  444.3 339.9 %reduce-scatter.8.cloned.1.call-start = ((), (), s32[]{:S(2)}) async-start(), calls=%async_computation.5 | async-start | bytes 17031168 | tf_op jit(solution)/shard_map/reduce_scatter | solution.py:135
  473.9 7.7 collective-permute-start.7
  475.2 9.9 %collective-permute-start.8 = (bf16[10,11,384]{2,1,0:T(8,128)(2,1)S(1)}, bf16[10,11,384]{2,1,0:T(8,128)(2,1)S(1)}, u32[]{:S(2)}, u32[]{:S(2)}) collective-permute-start(bf16[10,11,384]{2,1,0:T(8,128)(2,1)S(1)} %get-tuple-element.31), channel_id=1, source_target_pairs={{0,1},{1,2},{2,3},{4,5},{5,6},{6,7},{8,9},{9,10},{10,11},{12,13},{... | collective-permute-start | bytes 253448 | tf_op jit(solution)/shard_map/ppermute | solution.py:29
  536.0 13.1 %copy-start.25 = (f32[768]{0:T(1024)}, f32[768]{0:T(1024)S(1)}, u32[]{:S(2)}) copy-start(f32[768]{0:T(1024)S(1)} %get-tuple-element.16) | copy-start | bytes 9220
  536.0 13.1 %copy-start.26 = (f32[768]{0:T(1024)}, f32[768]{0:T(1024)S(1)}, u32[]{:S(2)}) copy-start(f32[768]{0:T(1024)S(1)} %get-tuple-element.17) | copy-start | bytes 9220
  (18 other events, 71.8 us)
Sparse Core Ops, SparseCore 0:
  10.8 58.2 all-gather.2
  72.0 79.8 all-gather.4
  380.7 98.3 reduce-scatter.11
  484.9 102.5 reduce-scatter.9
  594.3 189.8 reduce-scatter.7
